TPU v7x, 512 devices: a whole 4x8x8 slice. The times are simulated.
512 devices in a mesh: traj: 4 (over x), slab: 128 (over z, y, core).
Axes of the slice: x: 4, y: 8, z: 8, core: 2. Of those that a mesh axis runs over, the one named last changes fastest.
Arguments:
- grad_out: bfloat16 [1024, 384, 128], P(('traj', 'slab')), parts along dimension 0, may hold values from -96 to 96
- cached: bfloat16 [1024, 384, 128], P('traj', 'slab'), parts along dimension 0, may hold values from -0.059814453 to 0.059814453
- values: bfloat16 [1024, 384, 128], P(('traj', 'slab')), parts along dimension 0, may hold values from -0.75 to 0.75
- query_x: bfloat16 [1024, 128], P('traj'), parts along dimension 0, may hold values from -6 to 6
- key_x: bfloat16 [1024, 128], P('traj'), parts along dimension 0, may hold values from -6 to 6
- query_y: bfloat16 [1536, 128], P('traj'), parts along dimension 0, may hold values from -6 to 6
- key_y: bfloat16 [1536, 128], P('traj'), parts along dimension 0, may hold values from -6 to 6
Outputs:
- grad_values: bfloat16 [1024, 384, 128], P(('traj', 'slab')), parts along dimension 0
- query_x_grad: float32 [1024, 128], P(('traj', 'slab')), parts along dimension 0
- key_x_grad: float32 [1024, 128], P(('traj', 'slab')), parts along dimension 0
- query_y_grad: float32 [1536, 128], P(('traj', 'slab')), parts along dimension 0
- key_y_grad: float32 [1536, 128], P(('traj', 'slab')), parts along dimension 0
There are 4 independent parts, one for each index of `traj`. A program takes and returns all parts, laid end to end along the dimension named above; each array names one. Nothing has to cross between parts.
All inputs are finite; a program needn't handle non-finite values.
Results may differ from a plain program's by a relative error of at most 0.0067.
Values may be sent and summed in bfloat16 or wider, within the bound.
No kernel may reach another device: no remote copies, remote signals or barrier semaphores. Data moves between devices by JAX's collectives and lax.ppermute only.
A program may use at most 64 MiB of HBM per device.

v0:
```python
import math
import jax
import jax.numpy as jnp
from jax import lax
from jax.sharding import PartitionSpec as P

HEADS = 4
HEAD = 32


def axis_kernel(queries, key_rows):
    scores = jnp.dot(queries, key_rows.T, preferred_element_type=jnp.float32) / math.sqrt(HEAD)
    return jax.nn.softmax(scores, axis=1)


def local_terms(kernel, coupling, queries, key_rows):
    row_delta = jnp.sum(kernel * coupling, axis=1)
    weighted = kernel * coupling
    grad_query = jnp.dot(
        weighted, key_rows.astype(jnp.float32), precision=lax.Precision.HIGHEST
    ) / math.sqrt(HEAD)
    grad_key = jnp.dot(
        weighted.T, queries.astype(jnp.float32), precision=lax.Precision.HIGHEST
    ) / math.sqrt(HEAD)
    return (grad_query, grad_key, row_delta)


def corrections(own_rows, own_cols, delta_total, queries, key_rows, start, count):
    own_delta = lax.dynamic_slice_in_dim(delta_total, start, count, 0)
    query_fix = (
        own_delta[:, None]
        * jnp.dot(own_rows, key_rows.astype(jnp.float32), precision=lax.Precision.HIGHEST)
        / math.sqrt(HEAD)
    )
    key_fix = jnp.dot(
        own_cols.T,
        delta_total[:, None] * queries.astype(jnp.float32),
        precision=lax.Precision.HIGHEST,
    ) / math.sqrt(HEAD)
    return (query_fix, key_fix)


def on_device(grad_out, cached, values, query_x, key_x, query_y, key_y):
    index = lax.axis_index("slab")
    x_rows = grad_out.shape[0]
    x_count = cached.shape[0]
    y_rows = cached.shape[1]
    x_start = index * x_rows
    y_start = index * y_rows
    grad_columns = lax.all_to_all(grad_out, "slab", split_axis=1, concat_axis=0, tiled=True)
    mixed_heads = []
    query_terms = []
    key_terms = []
    delta_terms = []
    row_slices = []
    col_slices = []
    for head_index in range(HEADS):
        offset = head_index * HEAD
        head_query = query_x[:, offset : offset + HEAD]
        head_key = key_x[:, offset : offset + HEAD]
        kernel = axis_kernel(head_query, head_key)
        grad_rows = grad_columns[:, :, offset : offset + HEAD].reshape(x_count, y_rows * HEAD)
        saved_rows = cached[:, :, offset : offset + HEAD].reshape(x_count, y_rows * HEAD)
        grad_mixed = lax.dot_general(
            kernel.astype(jnp.bfloat16),
            grad_rows,
            (((0,), (0,)), ((), ())),
            preferred_element_type=jnp.float32,
        ).astype(jnp.bfloat16)
        coupling = lax.dot_general(
            grad_rows, saved_rows, (((1,), (1,)), ((), ())), preferred_element_type=jnp.float32
        )
        grad_query, grad_key, row_delta = local_terms(kernel, coupling, head_query, head_key)
        query_terms.append(grad_query)
        key_terms.append(grad_key)
        delta_terms.append(row_delta)
        row_slices.append(lax.dynamic_slice_in_dim(kernel, x_start, x_rows, 0))
        col_slices.append(lax.dynamic_slice_in_dim(kernel, x_start, x_rows, 1))
        mixed_heads.append(grad_mixed.reshape(x_count, y_rows, HEAD))
    mixed_rows = lax.all_to_all(
        jnp.concatenate(mixed_heads, axis=2), "slab", split_axis=0, concat_axis=1, tiled=True
    )
    x_delta_total = lax.psum(jnp.stack(delta_terms), "slab")
    query_x_grad, key_x_grad = (
        lax.psum_scatter(
            jnp.concatenate(query_terms, axis=1), "slab", scatter_dimension=0, tiled=True
        ),
        lax.psum_scatter(
            jnp.concatenate(key_terms, axis=1), "slab", scatter_dimension=0, tiled=True
        ),
    )
    query_fixes = []
    key_fixes = []
    for head_index in range(HEADS):
        offset = head_index * HEAD
        query_fix, key_fix = corrections(
            row_slices[head_index],
            col_slices[head_index],
            x_delta_total[head_index],
            query_x[:, offset : offset + HEAD],
            key_x[:, offset : offset + HEAD],
            x_start,
            x_rows,
        )
        query_fixes.append(query_fix)
        key_fixes.append(key_fix)
    query_x_grad = query_x_grad - jnp.concatenate(query_fixes, axis=1)
    key_x_grad = key_x_grad - jnp.concatenate(key_fixes, axis=1)
    value_heads = []
    query_terms = []
    key_terms = []
    delta_terms = []
    row_slices = []
    col_slices = []
    for head_index in range(HEADS):
        offset = head_index * HEAD
        head_query = query_y[:, offset : offset + HEAD]
        head_key = key_y[:, offset : offset + HEAD]
        kernel = axis_kernel(head_query, head_key)
        mixed_head = mixed_rows[:, :, offset : offset + HEAD]
        value_head = values[:, :, offset : offset + HEAD]
        grad_value = jnp.einsum(
            "jk,xje->xke",
            kernel.astype(jnp.bfloat16),
            mixed_head,
            preferred_element_type=jnp.float32,
        )
        coupling = jnp.einsum(
            "xje,xke->jk", mixed_head, value_head, preferred_element_type=jnp.float32
        )
        grad_query, grad_key, row_delta = local_terms(kernel, coupling, head_query, head_key)
        query_terms.append(grad_query)
        key_terms.append(grad_key)
        delta_terms.append(row_delta)
        row_slices.append(lax.dynamic_slice_in_dim(kernel, y_start, y_rows, 0))
        col_slices.append(lax.dynamic_slice_in_dim(kernel, y_start, y_rows, 1))
        value_heads.append(grad_value.astype(jnp.bfloat16))
    y_delta_total = lax.psum(jnp.stack(delta_terms), "slab")
    query_y_grad, key_y_grad = (
        lax.psum_scatter(
            jnp.concatenate(query_terms, axis=1), "slab", scatter_dimension=0, tiled=True
        ),
        lax.psum_scatter(
            jnp.concatenate(key_terms, axis=1), "slab", scatter_dimension=0, tiled=True
        ),
    )
    query_fixes = []
    key_fixes = []
    for head_index in range(HEADS):
        offset = head_index * HEAD
        query_fix, key_fix = corrections(
            row_slices[head_index],
            col_slices[head_index],
            y_delta_total[head_index],
            query_y[:, offset : offset + HEAD],
            key_y[:, offset : offset + HEAD],
            y_start,
            y_rows,
        )
        query_fixes.append(query_fix)
        key_fixes.append(key_fix)
    query_y_grad = query_y_grad - jnp.concatenate(query_fixes, axis=1)
    key_y_grad = key_y_grad - jnp.concatenate(key_fixes, axis=1)
    grad_values = jnp.concatenate(value_heads, axis=2)
    return (grad_values, query_x_grad, key_x_grad, query_y_grad, key_y_grad)


def solution(mesh):
    return jax.shard_map(
        on_device,
        mesh=mesh,
        in_specs=(
            P(("traj", "slab"), None, None),
            P("traj", "slab", None),
            P(("traj", "slab"), None, None),
            P("traj", None),
            P("traj", None),
            P("traj", None),
            P("traj", None),
        ),
        out_specs=(
            P(("traj", "slab"), None, None),
            P(("traj", "slab"), None),
            P(("traj", "slab"), None),
            P(("traj", "slab"), None),
            P(("traj", "slab"), None),
        ),
        check_vma=False,
    )
```

profile of v0, /device:TPU:24, one launch (start us, length us, event | category | flops | bytes accessed | tf_op | source)
XLA Modules:
  0.0 825.0 jit_solution(5174410356687245763)
XLA Ops:
  7.2 1.8 copy.95
  9.0 17.7 %all-to-all-start = ((bf16[2,384,128]{2,0,1:T(2,128)(2,1)}), bf16[2,384,128]{2,0,1:T(2,128)(2,1)}, u32[]{:S(2)}, u32[]{:S(2)}) async-start(bf16[2,384,128]{2,0,1:T(2,128)(2,1)} %copy.95), calls=%async_computation | async-start | bytes 393216 | tf_op jit(solution)/shard_map/all_to_all | solution.py:50
  26.7 1.0 fusion.169
  30.4 1.3 dynamic-slice.8
  33.0 1.1 fusion.39
  34.1 0.7 fusion.38
  34.9 0.7 fusion.36
  35.9 0.7 fusion.40
  37.9 1.1 copy.96
  39.0 1.8 fusion.177
  41.2 0.9 convolution_multiply_fusion.22
  42.1 0.8 fusion.178
  43.0 0.9 convolution_multiply_fusion.19
  43.8 0.8 convolution_multiply_fusion.23
  44.7 0.9 fusion.175
  45.6 0.9 convolution_multiply_fusion.16
  46.5 0.9 convolution_multiply_fusion.20
  47.4 1.0 fusion.165
  48.5 0.9 fusion.176
  49.4 0.7 copy-done.14
  50.1 0.9 convolution_multiply_fusion.21
  51.0 1.7 copy.148
  52.6 1.0 convolution_convert_fusion.7
  53.6 1.7 copy.150
  55.3 1.8 convolution_convert_fusion.5
  57.0 1.7 copy.149
  58.7 1.6 convolution_convert_fusion.6
  60.3 1.7 copy.151
  62.0 1.6 convolution_convert_fusion.4
  63.6 1.7 copy.104
  65.2 1.7 copy.102
  66.9 1.7 copy.103
  68.6 0.9 copy.101
  69.5 2.7 pad_maximum_fusion
  72.2 14.0 %all-to-all-start.1 = ((bf16[256,3,128]{2,1,0:T(4,128)(2,1)}), bf16[256,3,128]{2,1,0:T(4,128)(2,1)}, u32[]{:S(2)}, u32[]{:S(2)}) async-start(bf16[256,3,128]{2,1,0:T(4,128)(2,1)} %pad_maximum_fusion), calls=%async_computation.1 | async-start | bytes 524288 | tf_op jit(solution)/shard_map/all_to_all | solution.py:80
  86.4 1.5 pad_maximum_fusion.4
  90.0 0.7 pad_maximum_fusion.5
  90.6 8.0 all-to-all-done.1
  98.7 1.0 copy.105
  99.8 1.5 fusion.164
  101.3 1.1 copy.153
  102.4 0.9 fusion.9
  103.7 1.1 convolution_multiply_fusion.10
  104.9 1.0 convolution_multiply_fusion.14
  105.9 1.1 copy.152
  106.9 0.8 fusion.8
  108.2 1.1 convolution_multiply_fusion.11
  109.3 1.0 convolution_multiply_fusion.15
  110.2 1.1 copy.155
  111.3 0.9 fusion.11
  112.6 1.1 convolution_multiply_fusion.8
  113.7 1.0 convolution_multiply_fusion.12
  114.7 1.1 copy.154
  116.0 0.7 copy-done.12
  117.7 1.0 convolution_multiply_fusion.13
  118.7 0.7 pad_maximum_fusion.1
  119.4 1.7 copy.127
  121.2 0.7 copy-done.31
  121.8 478.3 %all-reduce.4 = (f32[4,256]{1,0:T(4,128)S(1)}, f32[4,384]{1,0:T(4,128)S(1)}) all-reduce(f32[4,256]{1,0:T(4,128)S(1)} %copy-done.31, f32[4,384]{1,0:T(4,128)S(1)} %pad_maximum_fusion.6), channel_id=1, replica_groups=mesh['traj'=4,'slab'=128] {'slab'}, use_global_device_ids=true, to_apply=%region_21.0 | all-reduce | flops 2560 | bytes 20480 | tf_op jit(solution)/shard_map/psum | solution.py:83
  600.5 0.8 convolution_multiply_fusion.35
  607.6 0.7 pad_maximum_fusion.2
  608.5 0.7 pad_maximum_fusion.3
  610.1 204.0 %all-reduce.8.cloned.1.call-done = (f32[256,128]{0,1:T(8,128)}, f32[256,128]{0,1:T(8,128)}, f32[384,128]{0,1:T(8,128)}, f32[384,128]{0,1:T(8,128)}) async-done(((f32[256,128]{0,1:T(8,128)}, f32[256,128]{0,1:T(8,128)}, f32[384,128]{0,1:T(8,128)}, f32[384,128]{0,1:T(8,128)}), (f32[256,128]{0,1:T(8,128)}, f32[256,128]{0,1:T(8,128)}, f32[384,128]{0,1:T(8,128)}, ...) | async-done | bytes 655376
  814.1 1.1 dynamic-slice_subtract_fusion
  (145 shorter events, 20.3 us)
Async XLA Ops:
  9.0 17.7 %copy-start.1 = (bf16[256,128]{1,0:T(8,128)(2,1)S(1)}, bf16[256,128]{1,0:T(8,128)(2,1)}, u32[]{:S(2)}) copy-start(bf16[256,128]{1,0:T(8,128)(2,1)} %param.11) | copy-start | bytes 196612
  9.0 17.7 %copy-start.3 = (bf16[256,128]{1,0:T(8,128)(2,1)S(1)}, bf16[256,128]{1,0:T(8,128)(2,1)}, u32[]{:S(2)}) copy-start(bf16[256,128]{1,0:T(8,128)(2,1)} %param.10) | copy-start | bytes 196612
  9.0 28.9 %all-to-all-start = ((bf16[2,384,128]{2,0,1:T(2,128)(2,1)}), bf16[2,384,128]{2,0,1:T(2,128)(2,1)}, u32[]{:S(2)}, u32[]{:S(2)}) async-start(bf16[2,384,128]{2,0,1:T(2,128)(2,1)} %copy.95), calls=%async_computation | async-start | bytes 393216 | tf_op jit(solution)/shard_map/all_to_all | solution.py:50
  28.2 0.9 copy-start
  28.2 0.9 copy-start.2
  33.0 1.1 copy-start.13
  37.5 1.5 copy-start.4
  40.8 1.2 copy-start.8
  41.2 1.0 copy-start.5
  47.4 1.0 copy-start.6
  49.4 0.7 copy-start.14
  72.2 14.2 %copy-start.28 = (f32[256,32]{0,1:T(8,128)S(1)}, f32[256,32]{0,1:T(8,128)}, u32[]{:S(2)}) copy-start(f32[256,32]{0,1:T(8,128)} %convolution_multiply_fusion.22) | copy-start | bytes 98308
  72.2 26.5 %all-to-all-start.1 = ((bf16[256,3,128]{2,1,0:T(4,128)(2,1)}), bf16[256,3,128]{2,1,0:T(4,128)(2,1)}, u32[]{:S(2)}, u32[]{:S(2)}) async-start(bf16[256,3,128]{2,1,0:T(4,128)(2,1)} %pad_maximum_fusion), calls=%async_computation.1 | async-start | bytes 524288 | tf_op jit(solution)/shard_map/all_to_all | solution.py:80
  86.1 728.0 %all-reduce.8.cloned.1.call-start = ((), (), s32[]{:S(2)}) async-start(), calls=%async_computation.2 | async-start | bytes 1310720
  86.4 1.5 copy-start.33
  86.4 1.5 copy-start.34
  86.4 1.5 copy-start.35
  86.4 2.8 copy-start.15
  87.9 0.7 copy-start.32
  89.2 0.8 copy-start.26
  89.2 0.8 copy-start.27
  102.4 0.9 copy-start.9
  106.9 0.9 copy-start.10
  111.3 0.9 copy-start.11
  115.8 0.9 copy-start.12
  117.6 1.1 copy-start.23
  117.6 1.1 copy-start.24
  117.6 1.1 copy-start.25
  121.2 0.7 copy-start.31
  600.4 1.6 copy-start.7
  606.5 0.8 copy-start.21
  606.5 0.8 copy-start.22
  606.7 0.8 copy-start.19
  606.8 0.8 copy-start.17
  607.6 0.8 copy-start.16
  607.6 0.8 copy-start.18
  607.6 0.9 copy-start.20
  609.3 0.7 copy-start.36
  815.2 1.3 copy-start.30
  816.5 0.9 copy-start.29
Sparse Core Ops, SparseCore 0:
  609.4 204.6 all-reduce.7
where the time goes:
time: 827 us; the launch traced here: 825 us
  blocking collectives  478 us (58%)
  waiting for transfers between devices  212 us (26%)
  matrix products  37.6 us (5%)
  local copies, waits for them, and re-layouts  35.5 us (4%)
  starting transfers between devices  31.9 us (4%)
  between operations  15.8 us (2%)
  other arithmetic  13.5 us (2%)
    psum x1, blocking collectives, on_device(): x_delta_total = lax.psum(jnp.stack(delta_terms), 'slab')  478 us
    unnamed x2, waiting for transfers between devices  204 us
    unnamed x90, local copies, waits for them, and re-layouts  24.8 us
    all_to_all x1, starting transfers between devices, on_device(): lax.all_to_all(grad_out, 'slab', split_axis=1, concat_axis=0, tiled=True)  17.7 us
  transfers between devices with their start and end apart: 3, of which 3 were waited for; matrix products, arithmetic and copies ran while one was open for 1% of the time, Pallas kernels for 0%

commit v1 on v0

--- a/solution.py
+++ b/solution.py
@@ -80,7 +80,7 @@
     mixed_rows = lax.all_to_all(
         jnp.concatenate(mixed_heads, axis=2), "slab", split_axis=0, concat_axis=1, tiled=True
     )
-    x_delta_total = lax.psum(jnp.stack(delta_terms), "slab")
+    x_delta_total = jnp.sum(lax.all_gather(jnp.stack(delta_terms), "slab"), axis=0)
     query_x_grad, key_x_grad = (
         lax.psum_scatter(
             jnp.concatenate(query_terms, axis=1), "slab", scatter_dimension=0, tiled=True

time: 827 us -> 617 us (0.75)
  blocking collectives: 478 us -> 293 us
  local copies, waits for them, and re-layouts: 35.5 us -> 19.9 us
    psum x1, blocking collectives: 478 us -> 238 us  [on_device(): y_delta_total = lax.psum(jnp.stack(delta_terms), 'slab')]
    all_gather x0 -> x1, blocking collectives: none -> 55 us  [on_device(): lax.all_gather(jnp.stack(delta_terms), 'slab')]
    unnamed x90 -> x88, local copies, waits for them, and re-layouts: 24.8 us -> 15.5 us
  transfers between devices with their start and end apart: 3 -> 3, of which waited for: 3 -> 3; matrix products, arithmetic and copies ran while one was open for 1% -> 2% of each run, Pallas kernels for 0% -> 0%
where the time goes in v1:
time: 617 us; the launch traced here: 616 us
  blocking collectives  293 us (47%)
  waiting for transfers between devices  214 us (35%)
  matrix products  31.2 us (5%)
  starting transfers between devices  28.6 us (5%)
  local copies, waits for them, and re-layouts  19.9 us (3%)
  between operations  15.9 us (3%)
  other arithmetic  13.2 us (2%)
    psum x1, blocking collectives, on_device(): y_delta_total = lax.psum(jnp.stack(delta_terms), 'slab')  238 us
    unnamed x2, waiting for transfers between devices  204 us
    all_gather x1, blocking collectives, on_device(): lax.all_gather(jnp.stack(delta_terms), 'slab')  55 us
    all_to_all x1, starting transfers between devices, on_device(): lax.all_to_all(grad_out, 'slab', split_axis=1, concat_axis=0, tiled=True)  17.7 us
    unnamed x88, local copies, waits for them, and re-layouts  15.5 us
  transfers between devices with their start and end apart: 3, of which 3 were waited for; matrix products, arithmetic and copies ran while one was open for 2% of the time, Pallas kernels for 0%

profile of v1, /device:TPU:24, one launch (start us, length us, event | category | flops | bytes accessed | tf_op | source)
XLA Modules:
  0.0 616.1 jit_solution(17706471264998881810)
XLA Ops:
  7.2 1.8 copy.95
  9.0 17.7 %all-to-all-start = ((bf16[2,384,128]{2,0,1:T(2,128)(2,1)}), bf16[2,384,128]{2,0,1:T(2,128)(2,1)}, u32[]{:S(2)}, u32[]{:S(2)}) async-start(bf16[2,384,128]{2,0,1:T(2,128)(2,1)} %copy.95), calls=%async_computation | async-start | bytes 393216 | tf_op jit(solution)/shard_map/all_to_all | solution.py:50
  27.0 0.9 fusion.170
  28.5 0.6 copy-done
  30.5 1.3 dynamic-slice.8
  33.1 1.0 fusion.38
  34.2 0.7 fusion.36
  35.1 0.7 fusion.42
  35.9 0.8 fusion.40
  37.9 1.1 copy.96
  39.4 0.9 convolution_multiply_fusion.18
  40.6 0.6 copy-done.5
  41.5 0.9 convolution_multiply_fusion.19
  42.4 0.8 convolution_multiply_fusion.23
  43.7 0.9 convolution_multiply_fusion.16
  44.6 0.9 convolution_multiply_fusion.20
  45.5 1.0 fusion.165
  46.9 0.7 copy-done.12
  47.6 0.9 convolution_multiply_fusion.21
  48.5 55.0 %all-gather.1 = f32[128,4,256]{2,1,0:T(4,128)} all-gather(f32[1,4,256]{2,1,0:T(4,128)S(1)} %maximum_bitcast_fusion), channel_id=2, replica_groups=mesh['traj'=4,'slab'=128] {'slab'}, dimensions={0}, use_global_device_ids=true | all-gather | bytes 528384 | tf_op jit(solution)/shard_map/all_gather | solution.py:83
  103.5 1.2 reduce_sum.165
  104.7 0.9 convolution_multiply_fusion.34
  105.7 0.8 convolution_multiply_fusion.35
  106.5 0.9 fusion.19
  107.4 0.9 fusion.18
  108.3 0.9 convolution_multiply_fusion.33
  109.2 0.9 convolution_multiply_fusion.32
  110.1 0.9 fusion.17
  111.0 0.9 fusion.16
  112.0 1.0 copy.148
  113.2 1.0 copy.150
  114.2 1.2 convolution_convert_fusion.5
  115.5 0.8 convolution_convert_fusion.6
  117.0 0.6 copy-done.18
  118.0 0.9 copy.101
  118.8 2.5 pad_maximum_fusion
  121.3 10.7 %all-to-all-start.1 = ((bf16[256,3,128]{2,1,0:T(4,128)(2,1)}), bf16[256,3,128]{2,1,0:T(4,128)(2,1)S(1)}, u32[]{:S(2)}, u32[]{:S(2)}) async-start(bf16[256,3,128]{2,1,0:T(4,128)(2,1)} %pad_maximum_fusion), calls=%async_computation.1 | async-start | bytes 524288 | tf_op jit(solution)/shard_map/all_to_all | solution.py:80
  132.4 0.7 pad_maximum_fusion.4
  133.2 0.6 copy-done.28
  134.9 0.7 pad_maximum_fusion.5
  135.5 9.4 %all-to-all-done.1 = bf16[256,3,128]{2,1,0:T(4,128)(2,1)S(1)} async-done(((bf16[256,3,128]{2,1,0:T(4,128)(2,1)}), bf16[256,3,128]{2,1,0:T(4,128)(2,1)S(1)}, u32[]{:S(2)}, u32[]{:S(2)}) %all-to-all-start.1) | async-done | bytes 196640 | tf_op jit(solution)/shard_map/all_to_all | solution.py:80
  145.1 0.8 fusion.164
  146.0 0.9 fusion.9
  147.4 1.1 convolution_multiply_fusion.10
  148.5 1.0 convolution_multiply_fusion.14
  149.6 0.8 fusion.8
  150.8 0.5 convolution_multiply_fusion.11
  152.0 0.4 fusion.179
  152.4 0.5 convolution_multiply_fusion.8
  153.6 0.4 fusion.180
  154.1 0.5 convolution_multiply_fusion.9
  155.4 0.8 copy.127
  156.3 238.2 %psum.7 = f32[4,384]{1,0:T(4,128)S(1)} all-reduce(f32[4,384]{1,0:T(4,128)S(1)} %pad_maximum_fusion.6), channel_id=1, replica_groups=mesh['traj'=4,'slab'=128] {'slab'}, use_global_device_ids=true, to_apply=%region_28.0 | all-reduce | flops 1536 | bytes 12288 | tf_op jit(solution)/shard_map/psum | solution.py:138
  395.9 0.4 fusion.14
  397.6 0.6 copy-done.17
  398.2 0.7 pad_maximum_fusion.2
  399.0 0.7 pad_maximum_fusion.3
  400.3 204.2 %all-reduce.7.cloned.1.call-done = (f32[256,128]{0,1:T(8,128)}, f32[256,128]{0,1:T(8,128)}, f32[384,128]{0,1:T(8,128)}, f32[384,128]{0,1:T(8,128)}) async-done(((f32[256,128]{0,1:T(8,128)}, f32[256,128]{0,1:T(8,128)}, f32[384,128]{0,1:T(8,128)}, f32[384,128]{0,1:T(8,128)}), (f32[256,128]{0,1:T(8,128)}, f32[256,128]{0,1:T(8,128)}, f32[384,128]{0,1:T(8,128)}, ...) | async-done | bytes 655376
  604.6 1.0 dynamic-slice_subtract_fusion.2
  605.5 0.6 copy.129
  606.3 0.6 copy.128
  606.9 1.1 dynamic-slice_subtract_fusion
  608.0 0.7 copy.131
  608.6 0.7 copy.130
  (145 shorter events, 15.4 us)
Async XLA Ops:
  9.0 17.7 %copy-start.1 = (bf16[256,128]{1,0:T(8,128)(2,1)S(1)}, bf16[256,128]{1,0:T(8,128)(2,1)}, u32[]{:S(2)}) copy-start(bf16[256,128]{1,0:T(8,128)(2,1)} %param.11) | copy-start | bytes 196612
  9.0 17.7 %copy-start.3 = (bf16[256,128]{1,0:T(8,128)(2,1)S(1)}, bf16[256,128]{1,0:T(8,128)(2,1)}, u32[]{:S(2)}) copy-start(bf16[256,128]{1,0:T(8,128)(2,1)} %param.10) | copy-start | bytes 196612
  9.0 28.9 %all-to-all-start = ((bf16[2,384,128]{2,0,1:T(2,128)(2,1)}), bf16[2,384,128]{2,0,1:T(2,128)(2,1)}, u32[]{:S(2)}, u32[]{:S(2)}) async-start(bf16[2,384,128]{2,0,1:T(2,128)(2,1)} %copy.95), calls=%async_computation | async-start | bytes 393216 | tf_op jit(solution)/shard_map/all_to_all | solution.py:50
  27.0 6.0 copy-start.11
  28.2 0.9 copy-start
  28.2 0.9 copy-start.2
  33.1 1.0 copy-start.10
  37.9 1.1 copy-start.8
  40.3 0.9 copy-start.5
  42.4 0.9 copy-start.4
  45.5 1.0 copy-start.6
  46.9 0.7 copy-start.12
  105.6 2.7 copy-start.7
  114.2 1.2 copy-start.15
  115.5 0.9 copy-start.14
  116.8 0.8 copy-start.18
  121.3 11.0 %copy-start.24 = (f32[256,32]{0,1:T(8,128)S(1)}, f32[256,32]{0,1:T(8,128)}, u32[]{:S(2)}) copy-start(f32[256,32]{0,1:T(8,128)} %convolution_multiply_fusion.23) | copy-start | bytes 98308
  121.3 11.0 %copy-start.25 = (f32[256,32]{0,1:T(8,128)S(1)}, f32[256,32]{0,1:T(8,128)}, u32[]{:S(2)}) copy-start(f32[256,32]{0,1:T(8,128)} %convolution_multiply_fusion.20) | copy-start | bytes 98308
  121.3 11.1 %copy-start.26 = (f32[256,32]{0,1:T(8,128)S(1)}, f32[256,32]{0,1:T(8,128)}, u32[]{:S(2)}) copy-start(f32[256,32]{0,1:T(8,128)} %convolution_multiply_fusion.21) | copy-start | bytes 98308
  121.3 11.7 %copy-start.32 = (f32[2,32]{1,0:T(2,128)S(1)}, f32[2,32]{1,0:T(2,128)}, u32[]{:S(2)}) copy-start(f32[2,32]{1,0:T(2,128)} %convolution_multiply_fusion.34) | copy-start | bytes 772
  121.3 11.7 %copy-start.33 = (f32[2,32]{1,0:T(2,128)S(1)}, f32[2,32]{1,0:T(2,128)}, u32[]{:S(2)}) copy-start(f32[2,32]{1,0:T(2,128)} %convolution_multiply_fusion.35) | copy-start | bytes 772
  121.3 11.7 %copy-start.34 = (f32[2,32]{1,0:T(2,128)S(1)}, f32[2,32]{1,0:T(2,128)}, u32[]{:S(2)}) copy-start(f32[2,32]{1,0:T(2,128)} %convolution_multiply_fusion.33) | copy-start | bytes 772
  121.3 11.7 %copy-start.35 = (f32[2,32]{1,0:T(2,128)S(1)}, f32[2,32]{1,0:T(2,128)}, u32[]{:S(2)}) copy-start(f32[2,32]{1,0:T(2,128)} %convolution_multiply_fusion.32) | copy-start | bytes 772
  121.3 23.6 %all-to-all-start.1 = ((bf16[256,3,128]{2,1,0:T(4,128)(2,1)}), bf16[256,3,128]{2,1,0:T(4,128)(2,1)S(1)}, u32[]{:S(2)}, u32[]{:S(2)}) async-start(bf16[256,3,128]{2,1,0:T(4,128)(2,1)} %pad_maximum_fusion), calls=%async_computation.1 | async-start | bytes 524288 | tf_op jit(solution)/shard_map/all_to_all | solution.py:80
  132.0 2.0 copy-start.13
  132.1 472.5 %all-reduce.7.cloned.1.call-start = ((), (), s32[]{:S(2)}) async-start(), calls=%async_computation.2 | async-start | bytes 1310720
  133.0 0.7 copy-start.28
  133.0 0.7 copy-start.29
  133.1 0.7 copy-start.30
  133.1 0.7 copy-start.31
  134.1 0.8 copy-start.21
  134.1 0.8 copy-start.22
  134.1 0.8 copy-start.23
  146.0 0.9 copy-start.9
  154.6 0.8 copy-start.19
  154.6 0.8 copy-start.20
  397.4 0.8 copy-start.17
  398.2 0.8 copy-start.16
  604.6 1.6 copy-start.27
Sparse Core Ops, SparseCore 0:
  399.8 204.6 all-reduce.6
